TPU v7x, 256 devices: a whole 4x4x8 slice. The times are simulated.
256 devices in a mesh: obs: 4 (over x_lo, core), pan: 64 (over x_hi, y, z).
Axes of the slice: x: 4 (x_hi: 2, x_lo: 2; x = x_hi * 2 + x_lo), y: 4, z: 8, core: 2. Of those that a mesh axis runs over, the one named last changes fastest.
Arguments:
- sources: bfloat16 [64, 4, 2048, 256], P('pan', None, 'obs'), may hold values from -16 to 16
- panel_places: float32 [64, 3, 2048], P('pan', None, 'obs'), may hold values from -8 to 8
- observer_places: float32 [3, 1024], P(None, 'obs'), may hold values from 20 to 60
- fraction: bfloat16 [1024, 64, 2048], P(None, 'pan', 'obs'), may hold values from 0 to 1
- delay_bins: int32 [8, 64, 16], P(None, 'pan', 'obs'), may hold values from 0 to 127
- segment_owner: int32 [64], replicated, may hold values from 0 to 63, each once
Outputs:
- pressure: float32 [384, 1024], P('pan', 'obs')
Inputs may be any that keep to these rules, and one draw needn't show every extreme that they name: segment_owner is a permutation of the time segments' owners.
All inputs are finite; a program needn't handle non-finite values.
Results may differ from a plain program's by a relative error of at most 0.003.
Values may be sent and summed in bfloat16 or wider, within the bound.
A program may use at most 64 MiB of HBM per device.

v0:
```python
import math
import jax
import jax.numpy as jnp
from jax import lax
from jax.sharding import PartitionSpec as P

MAXD = 127
OBLK = 128
PBLK = 128


def block_kernel(place_block, observer_group, frac_group, amplitude):
    separation = observer_group[:, :, None] - place_block[:, None, :]
    dist_sq = jnp.sum(separation * separation, axis=0)
    monopole = amplitude / jnp.sqrt(dist_sq)
    dipole = amplitude * separation / dist_sq
    kernel = jnp.concatenate([monopole[None], dipole], axis=0)
    weight = frac_group.astype(jnp.float32)
    lower_part = (kernel * (1.0 - weight)).astype(jnp.bfloat16)
    upper_part = (kernel * weight).astype(jnp.bfloat16)
    return jnp.stack([lower_part, upper_part], axis=0)


def placed_block(src_block, weights):
    products = jnp.einsum("cjs,gcoj->sgo", src_block, weights, preferred_element_type=jnp.float32)
    return jnp.pad(products[:, 0], ((0, 1), (0, 0))) + jnp.pad(products[:, 1], ((1, 0), (0, 0)))


def per_device(sources, panel_places, observer_places, fraction, delay_bins, segment_owner):
    local_panels = sources.shape[2]
    window = sources.shape[3]
    bins_total = window + MAXD + 1
    amplitude = 60.0 / math.sqrt(local_panels * lax.axis_size("obs") * lax.axis_size("pan"))
    local_blocks = local_panels // PBLK
    every_obs = lax.all_gather(observer_places, "obs", axis=1, tiled=True)
    obs_total = every_obs.shape[1]
    obs_blocks = obs_total // OBLK
    span = window + 1
    lead = MAXD
    padded_rows = lead + span + (bins_total - span)
    columns = [None] * obs_blocks
    for block_index in range(local_blocks):
        lo_col = block_index * PBLK
        src_block = sources[0, :, lo_col : lo_col + PBLK]
        place_block = panel_places[0, :, lo_col : lo_col + PBLK]
        frac_cols = fraction[:, 0, lo_col : lo_col + PBLK]
        weights = block_kernel(place_block, every_obs, frac_cols, amplitude)
        placed = placed_block(src_block, weights)
        padded = jnp.pad(placed, ((lead, padded_rows - lead - span), (0, 0)))
        for ob in range(obs_blocks):
            shift = delay_bins[ob, 0, block_index]
            piece = lax.dynamic_slice(padded, (lead - shift, ob * OBLK), (bins_total, OBLK))
            columns[ob] = piece if columns[ob] is None else columns[ob] + piece
    totals = jnp.concatenate(columns, axis=1)
    reduced = lax.psum_scatter(totals, "obs", scatter_dimension=1, tiled=True)
    segment_count = segment_owner.shape[0]
    seg_len = bins_total // segment_count
    arranged = reduced.reshape(segment_count, seg_len, reduced.shape[1])
    inverse = jnp.argsort(segment_owner)
    arranged = arranged[inverse]
    return halving_sum(arranged, "pan", (0, 3, 1, 4, 2, 5))


def halving_sum(data, axis, bit_order):
    count = data.shape[0]
    levels = count.bit_length() - 1
    me = lax.axis_index(axis)
    data = data.reshape((2,) * levels + data.shape[1:])
    remaining = list(range(levels - 1, -1, -1))
    for bit in bit_order:
        dim = remaining.index(bit)
        mine = me >> bit & 1
        low = lax.index_in_dim(data, 0, dim, keepdims=False)
        high = lax.index_in_dim(data, 1, dim, keepdims=False)
        keep = jnp.where(mine == 1, high, low)
        send = jnp.where(mine == 1, low, high)
        pairs = [(p, p ^ 1 << bit) for p in range(count)]
        data = keep + lax.ppermute(send, axis, pairs)
        remaining.pop(dim)
    return data


def solution(mesh):
    return jax.shard_map(
        per_device,
        mesh=mesh,
        in_specs=(
            P("pan", None, "obs", None),
            P("pan", None, "obs"),
            P(None, "obs"),
            P(None, "pan", "obs"),
            P(None, "pan", "obs"),
            P(),
        ),
        out_specs=P("pan", "obs"),
        check_vma=False,
    )
```

profile of v0, /device:TPU:8, one launch (start us, length us, event | category | flops | bytes accessed | tf_op | source)
XLA Modules:
  0.0 158.8 jit_solution(11911982236685478341)
XLA Ops:
  6.5 1.4 broadcast_subtract_fusion
  8.8 5.2 %all_gather.3 = f32[3,1024]{1,0:T(4,128)S(1)} all-gather(f32[3,256]{1,0:T(4,128)S(1)} %copy-done.10), channel_id=1, replica_groups=mesh['obs'=4,'pan'=64] {'obs'}, dimensions={1}, use_global_device_ids=true | all-gather | bytes 15360 | tf_op jit(solution)/shard_map/all_gather | solution.py:35
  15.2 1.0 fusion.39
  61.4 1.6 %slice_bitcast_fusion.3 = (f32[256,1024]{1,0:T(8,128)}, f32[256,1024]{1,0:T(8,128)}) fusion(f32[256,2,1024]{2,0,1:T(8,128)S(1)} %fusion.19), kind=kLoop, calls=%fused_computation.92 | loop fusion | bytes 4194304 | tf_op jit(solution)/shard_map/squeeze | solution.py:26
  64.1 1.6 slice_bitcast_fusion.5
  66.8 1.5 slice_bitcast_fusion.7
  68.5 1.0 copy-done.2
  70.0 1.0 copy-done.4
  71.6 1.0 copy-done.6
  72.9 1.2 pad_add_fusion.3
  74.1 2.0 %fusion.51 = f32[384,1024]{1,0:T(8,128)} fusion(s32[]{:T(128)S(6)} %select_n.213, f32[257,1024]{1,0:T(8,128)} %pad_add_fusion.3, s32[]{:T(128)S(6)} %select_n.214, f32[257,1024]{1,0:T(8,128)S(1)} %pad_add_fusion.2, s32[]{:T(128)S(6)} %select_n.215, f32[257,1024]{1,0:T(8,128)S(1)} %pad_add_fusion.1, s32[]{:T(128)S(6)} %select_n.216, ...), kind=kLoop, calls=%fused_computation.121 | loop fusion | flops 147455 | bytes 4407312
  76.1 1.0 fusion.55
  77.2 1.0 fusion.59
  78.2 1.0 fusion.63
  79.2 1.0 fusion.67
  80.3 1.0 fusion.71
  81.3 1.0 fusion.75
  82.3 1.0 fusion.79
  84.0 2.0 %sort.17 = (s32[64]{0:T(128)}, s32[64]{0:T(128)S(1)}) sort(s32[64]{0:T(128)S(1)} %copy-done.12, s32[64]{0:T(128)S(1)} %iota.4), dimensions={0}, to_apply=%region_5.6 | sort | flops 384 | bytes 1024 | tf_op jit(solution)/shard_map/jit(argsort)/sort | solution.py:59
  86.1 26.8 %reduce-scatter.2.cloned.1.call-done = f32[384,256]{1,0:T(8,128)} async-done(((f32[384,1024]{1,0:T(8,128)}), f32[384,256]{1,0:T(8,128)}) %reduce-scatter.2.cloned.1.call-update) | async-done | bytes 393232 | tf_op jit(solution)/shard_map/reduce_scatter | solution.py:55
  112.8 1.0 reshape.463
  115.0 1.8 %collective-permute-start = (f32[2,2,2,2,2,6,256]{6,4,3,2,1,0,5:T(2,128)S(1)}, f32[2,2,2,2,2,6,256]{6,4,3,2,1,0,5:T(2,128)S(1)}, u32[]{:S(2)}, u32[]{:S(2)}) collective-permute-start(f32[2,2,2,2,2,6,256]{6,4,3,2,1,0,5:T(2,128)S(1)} %bitcast.234), channel_id=1, source_target_pairs={{0,1},{1,0},{2,3},{3,2},{4,5},{5,4},{6,7},{7,6},{8,9},{9,8},{10,11... | collective-permute-start | bytes 589832 | tf_op jit(solution)/shard_map/ppermute | solution.py:78
  116.8 5.4 %collective-permute-done = f32[2,2,2,2,2,6,256]{6,4,3,2,1,0,5:T(2,128)S(1)} collective-permute-done((f32[2,2,2,2,2,6,256]{6,4,3,2,1,0,5:T(2,128)S(1)}, f32[2,2,2,2,2,6,256]{6,4,3,2,1,0,5:T(2,128)S(1)}, u32[]{:S(2)}, u32[]{:S(2)}) %collective-permute-start) | collective-permute-done | bytes 196640 | tf_op jit(solution)/shard_map/ppermute | solution.py:78
  123.1 4.1 %collective-permute-done.1 = f32[2,2,2,2,6,256]{5,3,2,1,0,4:T(2,128)S(1)} collective-permute-done((f32[2,2,2,2,6,256]{5,3,2,1,0,4:T(2,128)S(1)}, f32[2,2,2,2,6,256]{5,3,2,1,0,4:T(2,128)S(1)}, u32[]{:S(2)}, u32[]{:S(2)}) %collective-permute-start.1) | collective-permute-done | bytes 98336 | tf_op jit(solution)/shard_map/ppermute | solution.py:78
  127.4 2.6 %collective-permute-start.2 = (f32[2,2,2,6,256]{4,2,1,0,3:T(2,128)S(1)}, f32[2,2,2,6,256]{4,2,1,0,3:T(2,128)S(1)}, u32[]{:S(2)}, u32[]{:S(2)}) collective-permute-start(f32[2,2,2,6,256]{4,2,1,0,3:T(2,128)S(1)} %bitcast.235), channel_id=1, source_target_pairs={{0,2},{1,3},{2,0},{3,1},{4,6},{5,7},{6,4},{7,5},{8,10},{9,11},{10,... | collective-permute-start | bytes 147464 | tf_op jit(solution)/shard_map/ppermute | solution.py:78
  130.0 2.4 %collective-permute-done.2 = f32[2,2,2,6,256]{4,2,1,0,3:T(2,128)S(1)} collective-permute-done((f32[2,2,2,6,256]{4,2,1,0,3:T(2,128)S(1)}, f32[2,2,2,6,256]{4,2,1,0,3:T(2,128)S(1)}, u32[]{:S(2)}, u32[]{:S(2)}) %collective-permute-start.2) | collective-permute-done | bytes 49184 | tf_op jit(solution)/shard_map/ppermute | solution.py:78
  132.6 2.2 %collective-permute-start.3 = (f32[2,2,6,256]{3,1,0,2:T(2,128)S(1)}, f32[2,2,6,256]{3,1,0,2:T(2,128)S(1)}, u32[]{:S(2)}, u32[]{:S(2)}) collective-permute-start(f32[2,2,6,256]{3,1,0,2:T(2,128)S(1)} %fusion.87), channel_id=1, source_target_pairs={{0,16},{1,17},{2,18},{3,19},{4,20},{5,21},{6,22},{7,23},{8,24},{9,... | collective-permute-start | bytes 73736 | tf_op jit(solution)/shard_map/ppermute | solution.py:78
  134.8 3.2 %collective-permute-done.3 = f32[2,2,6,256]{3,1,0,2:T(2,128)S(1)} collective-permute-done((f32[2,2,6,256]{3,1,0,2:T(2,128)S(1)}, f32[2,2,6,256]{3,1,0,2:T(2,128)S(1)}, u32[]{:S(2)}, u32[]{:S(2)}) %collective-permute-start.3) | collective-permute-done | bytes 24608 | tf_op jit(solution)/shard_map/ppermute | solution.py:78
  138.1 6.3 %collective-permute-start.4 = (f32[2,6,256]{2,0,1:T(2,128)S(1)}, f32[2,6,256]{2,0,1:T(2,128)S(1)}, u32[]{:S(2)}, u32[]{:S(2)}) collective-permute-start(f32[2,6,256]{2,0,1:T(2,128)S(1)} %bitcast.236), channel_id=1, source_target_pairs={{0,4},{1,5},{2,6},{3,7},{4,0},{5,1},{6,2},{7,3},{8,12},{9,13},{10,... | collective-permute-start | bytes 36872 | tf_op jit(solution)/shard_map/ppermute | solution.py:78
  144.4 1.7 %collective-permute-done.4 = f32[2,6,256]{2,0,1:T(2,128)S(1)} collective-permute-done((f32[2,6,256]{2,0,1:T(2,128)S(1)}, f32[2,6,256]{2,0,1:T(2,128)S(1)}, u32[]{:S(2)}, u32[]{:S(2)}) %collective-permute-start.4) | collective-permute-done | bytes 12320 | tf_op jit(solution)/shard_map/ppermute | solution.py:78
  146.2 2.8 %collective-permute-start.5 = (f32[6,256]{1,0:T(8,128)S(1)}, f32[6,256]{1,0:T(8,128)S(1)}, u32[]{:S(2)}, u32[]{:S(2)}) collective-permute-start(f32[6,256]{1,0:T(8,128)S(1)} %bitcast.237), channel_id=1, source_target_pairs={{0,32},{1,33},{2,34},{3,35},{4,36},{5,37},{6,38},{7,39},{8,40},{9,... | collective-permute-start | bytes 18440 | tf_op jit(solution)/shard_map/ppermute | solution.py:78
  148.9 2.5 %collective-permute-done.5 = f32[6,256]{1,0:T(8,128)S(1)} collective-permute-done((f32[6,256]{1,0:T(8,128)S(1)}, f32[6,256]{1,0:T(8,128)S(1)}, u32[]{:S(2)}, u32[]{:S(2)}) %collective-permute-start.5) | collective-permute-done | bytes 6176 | tf_op jit(solution)/shard_map/ppermute | solution.py:78
  (70 shorter events, 14.1 us)
Async XLA Ops:
  6.5 1.6 copy-start.1
  6.5 106.3 %reduce-scatter.2.cloned.1.call-start = ((), (), s32[]{:S(2)}) async-start(), calls=%async_computation.1 | async-start | bytes 1966080 | tf_op jit(solution)/shard_map/reduce_scatter | solution.py:55
  8.1 0.7 copy-start.9
  8.1 0.7 copy-start.10
  15.2 1.1 copy-start.8
  58.1 1.2 copy-start.11
  68.3 1.2 copy-start.2
  68.3 1.5 copy-start.3
  69.8 1.2 copy-start.4
  69.8 1.5 copy-start.5
  71.4 1.2 copy-start.6
  71.4 1.5 copy-start.7
  74.1 2.0 %copy-start = (f32[257,1024]{1,0:T(8,128)S(1)}, f32[257,1024]{1,0:T(8,128)}, u32[]{:S(2)}) copy-start(f32[257,1024]{1,0:T(8,128)} %pad_add_fusion.3) | copy-start | bytes 3158020
  83.3 0.7 copy-start.12
  115.0 7.2 %collective-permute-start = (f32[2,2,2,2,2,6,256]{6,4,3,2,1,0,5:T(2,128)S(1)}, f32[2,2,2,2,2,6,256]{6,4,3,2,1,0,5:T(2,128)S(1)}, u32[]{:S(2)}, u32[]{:S(2)}) collective-permute-start(f32[2,2,2,2,2,6,256]{6,4,3,2,1,0,5:T(2,128)S(1)} %bitcast.234), channel_id=1, source_target_pairs={{0,1},{1,0},{2,3},{3,2},{4,5},{5,4},{6,7},{7,6},{8,9},{9,8},{10,11... | collective-permute-start | bytes 589832 | tf_op jit(solution)/shard_map/ppermute | solution.py:78
  122.5 4.7 %collective-permute-start.1 = (f32[2,2,2,2,6,256]{5,3,2,1,0,4:T(2,128)S(1)}, f32[2,2,2,2,6,256]{5,3,2,1,0,4:T(2,128)S(1)}, u32[]{:S(2)}, u32[]{:S(2)}) collective-permute-start(f32[2,2,2,2,6,256]{5,3,2,1,0,4:T(2,128)S(1)} %fusion.82), channel_id=1, source_target_pairs={{0,8},{1,9},{2,10},{3,11},{4,12},{5,13},{6,14},{7,15},{8,0},{9,1},... | collective-permute-start | bytes 294920 | tf_op jit(solution)/shard_map/ppermute | solution.py:78
  127.4 5.1 %collective-permute-start.2 = (f32[2,2,2,6,256]{4,2,1,0,3:T(2,128)S(1)}, f32[2,2,2,6,256]{4,2,1,0,3:T(2,128)S(1)}, u32[]{:S(2)}, u32[]{:S(2)}) collective-permute-start(f32[2,2,2,6,256]{4,2,1,0,3:T(2,128)S(1)} %bitcast.235), channel_id=1, source_target_pairs={{0,2},{1,3},{2,0},{3,1},{4,6},{5,7},{6,4},{7,5},{8,10},{9,11},{10,... | collective-permute-start | bytes 147464 | tf_op jit(solution)/shard_map/ppermute | solution.py:78
  132.6 5.4 %collective-permute-start.3 = (f32[2,2,6,256]{3,1,0,2:T(2,128)S(1)}, f32[2,2,6,256]{3,1,0,2:T(2,128)S(1)}, u32[]{:S(2)}, u32[]{:S(2)}) collective-permute-start(f32[2,2,6,256]{3,1,0,2:T(2,128)S(1)} %fusion.87), channel_id=1, source_target_pairs={{0,16},{1,17},{2,18},{3,19},{4,20},{5,21},{6,22},{7,23},{8,24},{9,... | collective-permute-start | bytes 73736 | tf_op jit(solution)/shard_map/ppermute | solution.py:78
  138.1 8.0 %collective-permute-start.4 = (f32[2,6,256]{2,0,1:T(2,128)S(1)}, f32[2,6,256]{2,0,1:T(2,128)S(1)}, u32[]{:S(2)}, u32[]{:S(2)}) collective-permute-start(f32[2,6,256]{2,0,1:T(2,128)S(1)} %bitcast.236), channel_id=1, source_target_pairs={{0,4},{1,5},{2,6},{3,7},{4,0},{5,1},{6,2},{7,3},{8,12},{9,13},{10,... | collective-permute-start | bytes 36872 | tf_op jit(solution)/shard_map/ppermute | solution.py:78
  146.2 5.2 %collective-permute-start.5 = (f32[6,256]{1,0:T(8,128)S(1)}, f32[6,256]{1,0:T(8,128)S(1)}, u32[]{:S(2)}, u32[]{:S(2)}) collective-permute-start(f32[6,256]{1,0:T(8,128)S(1)} %bitcast.237), channel_id=1, source_target_pairs={{0,32},{1,33},{2,34},{3,35},{4,36},{5,37},{6,38},{7,39},{8,40},{9,... | collective-permute-start | bytes 18440 | tf_op jit(solution)/shard_map/ppermute | solution.py:78
Sparse Core Ops, SparseCore 0:
  83.5 29.2 reduce-scatter.1
where the time goes:
time: 160 us; the launch traced here: 159 us
  between operations  54 us (34%)
  waiting for transfers between devices  46.1 us (29%)
  other arithmetic  19.8 us (12%)
  starting transfers between devices  16.4 us (10%)
  local copies, waits for them, and re-layouts  14.4 us (9%)
  blocking collectives  5.2 us (3%)
  matrix products  3.01 us (2%)
    reduce_scatter x1, waiting for transfers between devices, per_device(): reduced = lax.psum_scatter(totals, 'obs', scatter_dimension=1, tiled=True)  26.8 us
    ppermute x6, waiting for transfers between devices, halving_sum(): data = keep + lax.ppermute(send, axis, pairs)  19.3 us
    ppermute x6, starting transfers between devices, halving_sum(): data = keep + lax.ppermute(send, axis, pairs)  16.4 us
    unnamed x7, other arithmetic  8.21 us
    unnamed x32, local copies, waits for them, and re-layouts  6.32 us
    all_gather x1, blocking collectives, per_device(): every_obs = lax.all_gather(observer_places, 'obs', axis=1, tiled=True)  5.2 us
    squeeze x4, local copies, waits for them, and re-layouts, placed_block(): products[:, 0]  4.88 us
  transfers between devices with their start and end apart: 7, of which 7 were waited for; matrix products, arithmetic and copies ran while one was open for 1% of the time, Pallas kernels for 0%

commit v1 on v0

--- a/solution.py
+++ b/solution.py
@@ -32,7 +32,10 @@
     bins_total = window + MAXD + 1
     amplitude = 60.0 / math.sqrt(local_panels * lax.axis_size("obs") * lax.axis_size("pan"))
     local_blocks = local_panels // PBLK
-    every_obs = lax.all_gather(observer_places, "obs", axis=1, tiled=True)
+    devices = lax.axis_size("obs")
+    parts = jnp.stack([observer_places for _ in range(devices)])
+    parts = lax.all_to_all(parts, "obs", split_axis=0, concat_axis=0)
+    every_obs = jnp.concatenate(parts, axis=1)
     obs_total = every_obs.shape[1]
     obs_blocks = obs_total // OBLK
     span = window + 1

time: 160 us -> 148 us (0.925)
  local copies, waits for them, and re-layouts: 14.4 us -> 8.44 us
  other arithmetic: 19.8 us -> 14.3 us
  blocking collectives: 5.2 us -> 0 us
  starting transfers between devices: 16.4 us -> 19.6 us
    unnamed x7, other arithmetic: 8.21 us -> 2.46 us
    all_gather x1 -> x0, blocking collectives: 5.2 us -> none  [per_device(): every_obs = lax.all_gather(observer_places, 'obs', axis=1, tiled=True)]
    squeeze x4, local copies, waits for them, and re-layouts: 4.88 us -> 0.65 us  [placed_block(): products[:, 0]]
    all_to_all x0 -> x1, starting transfers between devices: none -> 3.24 us  [per_device(): parts = lax.all_to_all(parts, 'obs', split_axis=0, concat_axis=0)]
    unnamed x32 -> x26, local copies, waits for them, and re-layouts: 6.32 us -> 3.32 us
  transfers between devices with their start and end apart: 7 -> 8, of which waited for: 7 -> 7; matrix products, arithmetic and copies ran while one was open for 1% -> 5% of each run, Pallas kernels for 0% -> 0%
where the time goes in v1:
time: 148 us; the launch traced here: 147 us
  between operations  54.7 us (37%)
  waiting for transfers between devices  47.2 us (32%)
  starting transfers between devices  19.6 us (13%)
  other arithmetic  14.3 us (10%)
  local copies, waits for them, and re-layouts  8.44 us (6%)
  matrix products  3.01 us (2%)
    reduce_scatter x1, waiting for transfers between devices, per_device(): reduced = lax.psum_scatter(totals, 'obs', scatter_dimension=1, tiled=True)  27.8 us
    ppermute x6, waiting for transfers between devices, halving_sum(): data = keep + lax.ppermute(send, axis, pairs)  19.4 us
    ppermute x6, starting transfers between devices, halving_sum(): data = keep + lax.ppermute(send, axis, pairs)  16.4 us
    unnamed x26, local copies, waits for them, and re-layouts  3.32 us
    all_to_all x1, starting transfers between devices, per_device(): parts = lax.all_to_all(parts, 'obs', split_axis=0, concat_axis=0)  3.24 us
    dot_general x4, matrix products, placed_block(): jnp.einsum('cjs,gcoj->sgo', src_block, weights, preferred_element_type=jn...  3.01 us
  transfers between devices with their start and end apart: 8, of which 7 were waited for; matrix products, arithmetic and copies ran while one was open for 5% of the time, Pallas kernels for 0%

profile of v1, /device:TPU:8, one launch (start us, length us, event | category | flops | bytes accessed | tf_op | source)
XLA Modules:
  0.0 147.3 jit_solution(14445860175645228992)
XLA Ops:
  6.5 1.3 stack.10
  7.8 3.2 %all-to-all-start = ((f32[4,3,256]{2,1,0:T(4,128)}), f32[4,3,256]{2,1,0:T(4,128)S(1)}, u32[]{:S(2)}, u32[]{:S(2)}) async-start(f32[4,3,256]{2,1,0:T(4,128)} %stack.10), calls=%async_computation | async-start | bytes 32768 | tf_op jit(solution)/shard_map/all_to_all | solution.py:37
  11.1 2.4 %broadcast_subtract_fusion = (f32[1024,128]{1,0:T(8,128)}, f32[1024,128]{1,0:T(8,128)}, f32[1024,128]{1,0:T(8,128)S(1)}, f32[1024,128]{1,0:T(8,128)S(1)}) fusion(bf16[1024,1,512]{2,0,1:T(8,128)(2,1)} %param.9), kind=kLoop, calls=%fused_computation.114 | loop fusion | flops 1048576 | bytes 3145728 | tf_op jit(solution)/shard_map/sub | solution.py:19
  13.5 1.2 bitcast_convert_fusion
  14.7 0.7 fusion.104
  30.8 0.7 fusion.103
  57.0 1.0 fusion.37
  58.3 1.0 fusion.39
  59.8 0.9 copy-done.8
  60.7 0.8 fusion.16
  61.6 0.9 copy-done.1
  63.0 0.8 fusion.19
  64.3 0.8 fusion.22
  65.5 0.8 fusion.25
  70.2 1.2 copy-done.5
  71.4 2.0 %sort.17 = (s32[64]{0:T(128)}, s32[64]{0:T(128)S(1)}) sort(s32[64]{0:T(128)S(1)} %copy-done.9, s32[64]{0:T(128)S(1)} %iota.4), dimensions={0}, to_apply=%region_5.6 | sort | flops 384 | bytes 1024 | tf_op jit(solution)/shard_map/jit(argsort)/sort | solution.py:62
  73.5 27.8 %reduce-scatter.2.cloned.1.call-done = f32[384,256]{1,0:T(8,128)} async-done(((f32[384,1024]{1,0:T(8,128)}), f32[384,256]{1,0:T(8,128)}) %reduce-scatter.2.cloned.1.call-update) | async-done | bytes 393232 | tf_op jit(solution)/shard_map/reduce_scatter | solution.py:58
  101.3 1.0 reshape.469
  102.4 0.6 gather_fusion
  103.5 1.8 %collective-permute-start = (f32[2,2,2,2,2,6,256]{6,4,3,2,1,0,5:T(2,128)S(1)}, f32[2,2,2,2,2,6,256]{6,4,3,2,1,0,5:T(2,128)S(1)}, u32[]{:S(2)}, u32[]{:S(2)}) collective-permute-start(f32[2,2,2,2,2,6,256]{6,4,3,2,1,0,5:T(2,128)S(1)} %bitcast.237), channel_id=1, source_target_pairs={{0,1},{1,0},{2,3},{3,2},{4,5},{5,4},{6,7},{7,6},{8,9},{9,8},{10,11... | collective-permute-start | bytes 589832 | tf_op jit(solution)/shard_map/ppermute | solution.py:81
  105.3 5.4 %collective-permute-done = f32[2,2,2,2,2,6,256]{6,4,3,2,1,0,5:T(2,128)S(1)} collective-permute-done((f32[2,2,2,2,2,6,256]{6,4,3,2,1,0,5:T(2,128)S(1)}, f32[2,2,2,2,2,6,256]{6,4,3,2,1,0,5:T(2,128)S(1)}, u32[]{:S(2)}, u32[]{:S(2)}) %collective-permute-start) | collective-permute-done | bytes 196640 | tf_op jit(solution)/shard_map/ppermute | solution.py:81
  111.0 0.6 collective-permute-start.1
  111.6 4.1 %collective-permute-done.1 = f32[2,2,2,2,6,256]{5,3,2,1,0,4:T(2,128)S(1)} collective-permute-done((f32[2,2,2,2,6,256]{5,3,2,1,0,4:T(2,128)S(1)}, f32[2,2,2,2,6,256]{5,3,2,1,0,4:T(2,128)S(1)}, u32[]{:S(2)}, u32[]{:S(2)}) %collective-permute-start.1) | collective-permute-done | bytes 98336 | tf_op jit(solution)/shard_map/ppermute | solution.py:81
  115.9 2.6 %collective-permute-start.2 = (f32[2,2,2,6,256]{4,2,1,0,3:T(2,128)S(1)}, f32[2,2,2,6,256]{4,2,1,0,3:T(2,128)S(1)}, u32[]{:S(2)}, u32[]{:S(2)}) collective-permute-start(f32[2,2,2,6,256]{4,2,1,0,3:T(2,128)S(1)} %bitcast.240), channel_id=1, source_target_pairs={{0,2},{1,3},{2,0},{3,1},{4,6},{5,7},{6,4},{7,5},{8,10},{9,11},{10,... | collective-permute-start | bytes 147464 | tf_op jit(solution)/shard_map/ppermute | solution.py:81
  118.5 2.5 %collective-permute-done.2 = f32[2,2,2,6,256]{4,2,1,0,3:T(2,128)S(1)} collective-permute-done((f32[2,2,2,6,256]{4,2,1,0,3:T(2,128)S(1)}, f32[2,2,2,6,256]{4,2,1,0,3:T(2,128)S(1)}, u32[]{:S(2)}, u32[]{:S(2)}) %collective-permute-start.2) | collective-permute-done | bytes 49184 | tf_op jit(solution)/shard_map/ppermute | solution.py:81
  121.1 2.2 %collective-permute-start.3 = (f32[2,2,6,256]{3,1,0,2:T(2,128)S(1)}, f32[2,2,6,256]{3,1,0,2:T(2,128)S(1)}, u32[]{:S(2)}, u32[]{:S(2)}) collective-permute-start(f32[2,2,6,256]{3,1,0,2:T(2,128)S(1)} %fusion.87), channel_id=1, source_target_pairs={{0,16},{1,17},{2,18},{3,19},{4,20},{5,21},{6,22},{7,23},{8,24},{9,... | collective-permute-start | bytes 73736 | tf_op jit(solution)/shard_map/ppermute | solution.py:81
  123.3 3.2 %collective-permute-done.3 = f32[2,2,6,256]{3,1,0,2:T(2,128)S(1)} collective-permute-done((f32[2,2,6,256]{3,1,0,2:T(2,128)S(1)}, f32[2,2,6,256]{3,1,0,2:T(2,128)S(1)}, u32[]{:S(2)}, u32[]{:S(2)}) %collective-permute-start.3) | collective-permute-done | bytes 24608 | tf_op jit(solution)/shard_map/ppermute | solution.py:81
  126.6 6.3 %collective-permute-start.4 = (f32[2,6,256]{2,0,1:T(2,128)S(1)}, f32[2,6,256]{2,0,1:T(2,128)S(1)}, u32[]{:S(2)}, u32[]{:S(2)}) collective-permute-start(f32[2,6,256]{2,0,1:T(2,128)S(1)} %bitcast.241), channel_id=1, source_target_pairs={{0,4},{1,5},{2,6},{3,7},{4,0},{5,1},{6,2},{7,3},{8,12},{9,13},{10,... | collective-permute-start | bytes 36872 | tf_op jit(solution)/shard_map/ppermute | solution.py:81
  132.9 1.7 %collective-permute-done.4 = f32[2,6,256]{2,0,1:T(2,128)S(1)} collective-permute-done((f32[2,6,256]{2,0,1:T(2,128)S(1)}, f32[2,6,256]{2,0,1:T(2,128)S(1)}, u32[]{:S(2)}, u32[]{:S(2)}) %collective-permute-start.4) | collective-permute-done | bytes 12320 | tf_op jit(solution)/shard_map/ppermute | solution.py:81
  134.7 2.8 %collective-permute-start.5 = (f32[6,256]{1,0:T(8,128)S(1)}, f32[6,256]{1,0:T(8,128)S(1)}, u32[]{:S(2)}, u32[]{:S(2)}) collective-permute-start(f32[6,256]{1,0:T(8,128)S(1)} %bitcast.242), channel_id=1, source_target_pairs={{0,32},{1,33},{2,34},{3,35},{4,36},{5,37},{6,38},{7,39},{8,40},{9,... | collective-permute-start | bytes 18440 | tf_op jit(solution)/shard_map/ppermute | solution.py:81
  137.4 2.5 %collective-permute-done.5 = f32[6,256]{1,0:T(8,128)S(1)} collective-permute-done((f32[6,256]{1,0:T(8,128)S(1)}, f32[6,256]{1,0:T(8,128)S(1)}, u32[]{:S(2)}, u32[]{:S(2)}) %collective-permute-start.5) | collective-permute-done | bytes 6176 | tf_op jit(solution)/shard_map/ppermute | solution.py:81
  139.9 0.6 fusion.93
  (66 shorter events, 7.4 us)
Async XLA Ops:
  7.8 49.2 %all-to-all-start = ((f32[4,3,256]{2,1,0:T(4,128)}), f32[4,3,256]{2,1,0:T(4,128)S(1)}, u32[]{:S(2)}, u32[]{:S(2)}) async-start(f32[4,3,256]{2,1,0:T(4,128)} %stack.10), calls=%async_computation | async-start | bytes 32768 | tf_op jit(solution)/shard_map/all_to_all | solution.py:37
  11.1 2.5 %copy-start = (bf16[1024,1,512]{2,0,1:T(8,128)(2,1)S(1)}, bf16[1024,1,512]{2,0,1:T(8,128)(2,1)}, u32[]{:S(2)}) copy-start(bf16[1024,1,512]{2,0,1:T(8,128)(2,1)} %param.9) | copy-start | bytes 3145732
  11.1 90.2 %reduce-scatter.2.cloned.1.call-start = ((), (), s32[]{:S(2)}) async-start(), calls=%async_computation.2 | async-start | bytes 1966080 | tf_op jit(solution)/shard_map/reduce_scatter | solution.py:58
  13.5 1.2 copy-start.6
  13.5 18.0 %copy-start.7 = (f32[1,3,512]{2,0,1:T(1,128)S(1)}, f32[1,3,512]{2,0,1:T(1,128)}, u32[]{:S(2)}) copy-start(f32[1,3,512]{2,0,1:T(1,128)} %param.7) | copy-start | bytes 18436
  58.3 1.1 copy-start.3
  58.3 1.2 copy-start.4
  59.5 1.2 copy-start.8
  61.5 1.0 copy-start.1
  61.5 1.2 copy-start.2
  70.2 1.2 copy-start.5
  70.2 1.2 copy-start.9
  103.5 7.2 %collective-permute-start = (f32[2,2,2,2,2,6,256]{6,4,3,2,1,0,5:T(2,128)S(1)}, f32[2,2,2,2,2,6,256]{6,4,3,2,1,0,5:T(2,128)S(1)}, u32[]{:S(2)}, u32[]{:S(2)}) collective-permute-start(f32[2,2,2,2,2,6,256]{6,4,3,2,1,0,5:T(2,128)S(1)} %bitcast.237), channel_id=1, source_target_pairs={{0,1},{1,0},{2,3},{3,2},{4,5},{5,4},{6,7},{7,6},{8,9},{9,8},{10,11... | collective-permute-start | bytes 589832 | tf_op jit(solution)/shard_map/ppermute | solution.py:81
  111.0 4.7 %collective-permute-start.1 = (f32[2,2,2,2,6,256]{5,3,2,1,0,4:T(2,128)S(1)}, f32[2,2,2,2,6,256]{5,3,2,1,0,4:T(2,128)S(1)}, u32[]{:S(2)}, u32[]{:S(2)}) collective-permute-start(f32[2,2,2,2,6,256]{5,3,2,1,0,4:T(2,128)S(1)} %fusion.82), channel_id=1, source_target_pairs={{0,8},{1,9},{2,10},{3,11},{4,12},{5,13},{6,14},{7,15},{8,0},{9,1},... | collective-permute-start | bytes 294920 | tf_op jit(solution)/shard_map/ppermute | solution.py:81
  115.9 5.1 %collective-permute-start.2 = (f32[2,2,2,6,256]{4,2,1,0,3:T(2,128)S(1)}, f32[2,2,2,6,256]{4,2,1,0,3:T(2,128)S(1)}, u32[]{:S(2)}, u32[]{:S(2)}) collective-permute-start(f32[2,2,2,6,256]{4,2,1,0,3:T(2,128)S(1)} %bitcast.240), channel_id=1, source_target_pairs={{0,2},{1,3},{2,0},{3,1},{4,6},{5,7},{6,4},{7,5},{8,10},{9,11},{10,... | collective-permute-start | bytes 147464 | tf_op jit(solution)/shard_map/ppermute | solution.py:81
  121.1 5.4 %collective-permute-start.3 = (f32[2,2,6,256]{3,1,0,2:T(2,128)S(1)}, f32[2,2,6,256]{3,1,0,2:T(2,128)S(1)}, u32[]{:S(2)}, u32[]{:S(2)}) collective-permute-start(f32[2,2,6,256]{3,1,0,2:T(2,128)S(1)} %fusion.87), channel_id=1, source_target_pairs={{0,16},{1,17},{2,18},{3,19},{4,20},{5,21},{6,22},{7,23},{8,24},{9,... | collective-permute-start | bytes 73736 | tf_op jit(solution)/shard_map/ppermute | solution.py:81
  126.6 8.0 %collective-permute-start.4 = (f32[2,6,256]{2,0,1:T(2,128)S(1)}, f32[2,6,256]{2,0,1:T(2,128)S(1)}, u32[]{:S(2)}, u32[]{:S(2)}) collective-permute-start(f32[2,6,256]{2,0,1:T(2,128)S(1)} %bitcast.241), channel_id=1, source_target_pairs={{0,4},{1,5},{2,6},{3,7},{4,0},{5,1},{6,2},{7,3},{8,12},{9,13},{10,... | collective-permute-start | bytes 36872 | tf_op jit(solution)/shard_map/ppermute | solution.py:81
  134.7 5.2 %collective-permute-start.5 = (f32[6,256]{1,0:T(8,128)S(1)}, f32[6,256]{1,0:T(8,128)S(1)}, u32[]{:S(2)}, u32[]{:S(2)}) collective-permute-start(f32[6,256]{1,0:T(8,128)S(1)} %bitcast.242), channel_id=1, source_target_pairs={{0,32},{1,33},{2,34},{3,35},{4,36},{5,37},{6,38},{7,39},{8,40},{9,... | collective-permute-start | bytes 18440 | tf_op jit(solution)/shard_map/ppermute | solution.py:81
Sparse Core Ops, SparseCore 0:
  71.5 29.7 reduce-scatter.1
